TPU v7x, 32 devices: a whole 2x2x4 slice. The times are simulated.
32 devices in a mesh: aa: 8 (over y, x, core), ba: 4 (over z).
Axes of the slice: x: 2, y: 2, z: 4, core: 2. Of those that a mesh axis runs over, the one named last changes fastest.
Arguments:
- fast_query: bfloat16 [2, 2048, 5120], P(None, 'aa', 'ba'), may hold values from -6 to 6
- fast_key: bfloat16 [2, 2048, 5120], P(None, 'aa', 'ba'), may hold values from -6 to 6
- fast_value: bfloat16 [2, 2048, 5120], P(None, 'aa', 'ba'), may hold values from -6 to 6
- rates: float32 [2, 2048, 24], P(None, 'aa', 'ba'), may hold values from 5e-05 to 0.0005
- attn_query: bfloat16 [2, 2048, 5120], P(None, 'aa', 'ba'), may hold values from -4.5 to 4.5
- attn_key: bfloat16 [2, 2048, 5120], P(None, 'aa', 'ba'), may hold values from -4.5 to 4.5
- attn_value: bfloat16 [2, 2048, 5120], P(None, 'aa', 'ba'), may hold values from -6 to 6
- fast_weights: float32 [640, 3, 8, 640], P('aa', None, 'ba'), may hold values from -0.2814427 to 0.2814427
- gain: float32 [5120], replicated, may hold values from 0.5 to 1.5
Outputs:
- mixed: bfloat16 [2, 2048, 5120], P(None, ('aa', 'ba'))
- weights_out: float32 [640, 3, 8, 640], P('aa', None, 'ba')
- moment_out: float32 [640, 3, 8, 640], P('aa', None, 'ba')
All inputs are finite; a program needn't handle non-finite values.
Results may differ from a plain program's by a relative error of at most 0.028.
Values may be sent and summed in bfloat16 or wider, within the bound.
A program may use at most 192 MiB of HBM per device.

v0:
```python
import functools
import math

import jax
import jax.numpy as jnp
from jax import lax
from jax.experimental import pallas as pl
from jax.experimental.pallas import tpu as pltpu
from jax.sharding import PartitionSpec as P

AD = 128
WINDOW = 512


BETA = 0.9
EPS = 1e-06


def shift(x, axis, by):
    length = lax.axis_size(axis)
    return lax.ppermute(x, axis, [(i, (i + by) % length) for i in range(length)])


def activation(x):
    sig = jax.nn.sigmoid(x)
    return (x * sig, sig * (1.0 + x * (1.0 - sig)))


def project(x, w):
    return jnp.einsum("nhd,hfd->nhf", x, w, preferred_element_type=jnp.float32)


def forward(w, query):
    rows, heads = query.shape[0], w.shape[1]
    q = query.reshape(rows, heads, -1)
    act_q, _ = activation(project(q, w[0]))
    hidden_q = (act_q * project(q, w[1])).astype(jnp.bfloat16)
    return jnp.einsum("nhf,hfd->nhd", hidden_q, w[2], preferred_element_type=jnp.float32).reshape(
        rows, -1
    )


def partial_grads(w, key, value, rate):
    rows, heads = key.shape[0], w.shape[1]
    k = key.reshape(rows, heads, -1)
    v = value.reshape(rows, heads, -1)
    gate_in = project(k, w[0])
    up_in = project(k, w[1])
    back_in = project(v, w[2])
    act, slope = activation(gate_in)
    gate_x = (rate[..., 0:1] * (-back_in * up_in * slope)).astype(jnp.bfloat16)
    up_x = (rate[..., 1:2] * (-back_in * act)).astype(jnp.bfloat16)
    down_x = (rate[..., 2:3] * -(act * up_in)).astype(jnp.bfloat16)

    def part(left, right):
        return jnp.einsum("nhf,nhd->hfd", left, right, preferred_element_type=jnp.float32)

    return jnp.stack([part(gate_x, k), part(up_x, k), part(down_x, v)]).astype(jnp.bfloat16)


def attend_kernel(rows, groups, q_ref, *refs):
    out_ref = refs[-1]
    stretch = pl.program_id(0)
    base = stretch * (rows * groups) + lax.axis_index("aa") * rows
    q = q_ref[0]
    scores = []
    blocks = (len(refs) - 1) // 2
    row = lax.broadcasted_iota(jnp.int32, (rows, rows), 0)
    col = lax.broadcasted_iota(jnp.int32, (rows, rows), 1)
    for back in range(blocks):
        s = lax.dot_general(
            q, refs[back][0], (((1,), (1,)), ((), ())), preferred_element_type=jnp.float32
        ) / math.sqrt(AD)
        gap = row - col + back * rows
        ok = (gap >= 0) & (gap < WINDOW) & (col >= back * rows - base)
        scores.append(jnp.where(ok, s, -1e30))
    top = functools.reduce(jnp.maximum, [jnp.max(s, -1, keepdims=True) for s in scores])
    total = 0.0
    acc = 0.0
    for back in range(blocks):
        p = jnp.exp(scores[back] - top)
        total = total + jnp.sum(p, -1, keepdims=True)
        acc = acc + jnp.dot(
            p.astype(jnp.bfloat16), refs[blocks + back][0], preferred_element_type=jnp.float32
        )
    out_ref[0] = acc / total


def attend(q, keys, values):
    stretches, rows, width = q.shape
    groups = lax.axis_size("aa")
    own = pl.BlockSpec((1, rows, AD), lambda s, h: (s, 0, h))
    index = lax.axis_index("aa")

    def moved(x, back):
        if not back:
            return x
        return jnp.where(index < back, jnp.concatenate([x[:1], x[:-1]], 0), x)

    keys = [moved(x, b) for b, x in enumerate(keys)]
    values = [moved(x, b) for b, x in enumerate(values)]
    return pl.pallas_call(
        functools.partial(attend_kernel, rows, groups),
        grid=(stretches, width // AD),
        in_specs=[own] * (1 + 2 * len(keys)),
        out_specs=own,
        out_shape=jax.ShapeDtypeStruct(q.shape, jnp.float32),
        cost_estimate=pl.CostEstimate(
            flops=4 * stretches * rows * rows * len(keys) * width,
            bytes_accessed=40 * q.size,
            transcendentals=stretches * rows * rows * len(keys) * width // AD,
        ),
        name="attend",
    )(q, *keys, *values)


def sum_kernel(n, x_ref, out_ref, land, send_sem, recv_sem):
    me = lax.axis_index("aa")
    barrier = pltpu.get_barrier_semaphore()
    for step in range(1, n):
        pl.semaphore_signal(
            barrier,
            inc=1,
            device_id={"aa": lax.rem(me + step, n)},
            device_id_type=pl.DeviceIdType.MESH,
        )
    pl.semaphore_wait(barrier, n - 1)
    copies = []
    for step in range(1, n):
        copy = pltpu.make_async_remote_copy(
            src_ref=x_ref,
            dst_ref=land.at[step],
            send_sem=send_sem.at[step],
            recv_sem=recv_sem.at[step],
            device_id={"aa": lax.rem(me + step, n)},
            device_id_type=pl.DeviceIdType.MESH,
        )
        copy.start()
        copies.append(copy)
    total = x_ref[...]
    for step in range(1, n):
        copies[step - 1].wait_recv()
        total = total + land[step]
    for copy in copies:
        copy.wait_send()
    out_ref[...] = total


def sum_over(x):
    n = lax.axis_size("aa")
    vmem = pl.BlockSpec(memory_space=pltpu.VMEM)
    return pl.pallas_call(
        functools.partial(sum_kernel, n),
        in_specs=[vmem],
        out_specs=vmem,
        out_shape=jax.ShapeDtypeStruct(x.shape, x.dtype),
        scratch_shapes=[
            pltpu.VMEM((n,) + x.shape, x.dtype),
            pltpu.SemaphoreType.DMA((n,)),
            pltpu.SemaphoreType.DMA((n,)),
        ],
        compiler_params=pltpu.CompilerParams(collective_id=1, has_side_effects=True),
        name="sum_over",
    )(x)


def tie(values, anchor):
    out = lax.optimization_barrier(tuple(values) + (anchor,))
    return out[:-1], out[-1]


def local(
    fast_query, fast_key, fast_value, rates, attn_query, attn_key, attn_value, fast_weights, gain
):
    stretches, rows, width = fast_query.shape
    local_rows = fast_weights.shape[0]
    heads = fast_weights.shape[2]
    rate = rates.reshape(stretches, rows, heads, 3)
    index = lax.axis_index("aa")
    groups = lax.axis_size("aa")
    first_row = index * local_rows

    shard = jnp.transpose(fast_weights, (1, 2, 0, 3))
    wb = lax.all_gather(shard.astype(jnp.bfloat16), "aa", axis=2, tiled=True)
    (attn_key, attn_value), wb = tie((attn_key, attn_value), wb)
    far = [shift(attn_key, "aa", 2), shift(attn_value, "aa", 2)]

    full = wb.astype(jnp.float32)
    target = jnp.sqrt(jnp.sum(full * full, 2, keepdims=True) + EPS)
    gp = partial_grads(wb, fast_key[0], fast_value[0], rate[0])
    grads = lax.psum(gp, "aa").astype(jnp.float32)

    (fq,), _ = tie((fast_query,), gp)
    out0 = forward(wb, fq[0])
    far, out0 = tie(far, out0)
    odd = index % 2 == 1
    swap = [(i, i ^ 1) for i in range(groups)]
    near = [
        lax.ppermute(jnp.where(odd, f, o), "aa", swap) for f, o in zip(far, (attn_key, attn_value))
    ]
    attention = attend(
        attn_query, [attn_key, near[0], far[0]], [attn_value, near[1], far[1]]
    )
    (attention,), grads = tie((attention,), grads)

    trial = full - grads
    updated = trial * (target / jnp.sqrt(jnp.sum(trial * trial, 2, keepdims=True) + EPS))
    ub = updated.astype(jnp.bfloat16)
    gp1 = partial_grads(ub, fast_key[1], fast_value[1], rate[1])
    grads1 = lax.psum_scatter(gp1, "aa", scatter_dimension=2, tiled=True).astype(jnp.float32)
    (fq1,), _ = tie((fast_query,), gp1)
    out1 = forward(ub, fq1[1])
    combined = (jnp.stack([out0, out1]) + attention).astype(jnp.bfloat16)

    moment = BETA * lax.dynamic_slice_in_dim(grads, first_row, local_rows, 2) + grads1
    own = lax.dynamic_slice_in_dim(updated, first_row, local_rows, 2)
    trial = own - moment
    squares = sum_over(jnp.sum(trial * trial, 2).reshape(-1, trial.shape[3]))
    squares = squares.reshape(trial.shape[:2] + (1, trial.shape[3]))
    weights = trial * (target / jnp.sqrt(squares + EPS))

    arrived = lax.all_to_all(combined, "ba", split_axis=1, concat_axis=2, tiled=True)
    values = arrived.astype(jnp.float32)
    scale = lax.rsqrt(jnp.mean(values * values, -1, keepdims=True) + EPS)
    mixed = (values * scale * gain).astype(jnp.bfloat16)
    back = (2, 0, 1, 3)
    return (mixed, jnp.transpose(weights, back), jnp.transpose(moment, back))


def solution(mesh):
    token = P(None, "aa", "ba")
    hidden = P("aa", None, "ba", None)
    return jax.shard_map(
        local,
        mesh=mesh,
        in_specs=(token,) * 7 + (hidden, P()),
        out_specs=(P(None, ("aa", "ba"), None), hidden, hidden),
        check_vma=False,
    )
```

profile of v0, /device:TPU:0, one launch (start us, length us, event | category | flops | bytes accessed | tf_op | source)
XLA Modules:
  0.0 327.7 jit_solution(3080123507557281375)
XLA Ops:
  7.2 2.3 copy.235
  12.4 40.4 %all-gather.2.cloned.1.call-done = bf16[3,2,640,640]{3,2,1,0:T(8,128)(2,1)} async-done(((bf16[3,2,80,640]{3,2,1,0:T(8,128)(2,1)}), bf16[3,2,640,640]{3,2,1,0:T(8,128)(2,1)}) %all-gather.2.cloned.1.call-update) | async-done | bytes 4915216 | tf_op jit(solution)/shard_map/all_gather | solution.py:184
  52.8 2.1 fusion.46
  54.9 2.1 fusion.52
  57.1 2.2 fusion.43
  59.3 1.5 collective-permute-start
  60.8 1.3 collective-permute-start.1
  65.0 2.8 pad_maximum_fusion
  67.8 1.2 copy-done.1
  69.1 1.4 copy.167
  72.5 3.6 %fusion.49 = f32[256,2,640]{0,2,1:T(8,128)} fusion(bf16[256,2,640]{0,2,1:T(8,128)(2,1)S(1)} %bitcast.184, bf16[3,2,640,640]{3,2,1,0:T(8,128)(2,1)} %all-gather.2.cloned.1.call-done), kind=kOutput, calls=%fused_computation.60 | convolution fusion | flops 419430400 | bytes 3604480 | tf_op jit(solution)/shard_map/nhd,hfd->nhf/dot_general | solution.py:30
  76.1 5.0 %fusion.11 = f32[2,640,256]{2,1,0:T(8,128)} fusion(bf16[3,2,640,640]{3,2,1,0:T(8,128)(2,1)} %all-gather.2.cloned.1.call-done, bf16[256,2,640]{0,2,1:T(8,128)(2,1)} %bitcast.185, f32[256,2,640]{0,2,1:T(8,128)} %fusion.49), kind=kOutput, calls=%fused_computation.28 | convolution fusion | flops 840826880 | bytes 6553600 | tf_op jit(solution)/shard_map/nhf,hfd->nhd/dot_general | solution.py:38
  81.0 2.8 copy.212
  83.9 23.5 %collective-permute-done = bf16[2,256,1280]{2,1,0:T(8,128)(2,1)} collective-permute-done((bf16[2,256,1280]{2,1,0:T(8,128)(2,1)S(1)}, bf16[2,256,1280]{2,1,0:T(8,128)(2,1)}, u32[]{:S(2)}, u32[]{:S(2)}) %collective-permute-start) | collective-permute-done | bytes 1310752 | tf_op jit(solution)/shard_map/ppermute | solution.py:21
  107.4 38.4 %collective-permute-done.1 = bf16[2,256,1280]{2,1,0:T(8,128)(2,1)} collective-permute-done((bf16[2,256,1280]{2,1,0:T(8,128)(2,1)}, bf16[2,256,1280]{2,1,0:T(8,128)(2,1)}, u32[]{:S(2)}, u32[]{:S(2)}) %collective-permute-start.1) | collective-permute-done | bytes 1310752 | tf_op jit(solution)/shard_map/ppermute | solution.py:21
  145.8 1.2 slice.95
  147.0 1.1 slice.97
  148.1 3.5 %maximum_select_fusion.3 = (bf16[2,256,1280]{2,1,0:T(8,128)(2,1)}, bf16[2,256,1280]{2,1,0:T(8,128)(2,1)}) fusion(bf16[2,256,1280]{2,1,0:T(8,128)(2,1)} %collective-permute-done.1, bf16[1,256,1280]{2,1,0:T(8,128)(2,1)S(1)} %slice.97, pred[]{:T(512)S(6)} %lt.20, bf16[2,256,1280]{2,1,0:T(8,128)(2,1)} %refs_3_, pred[]{:T(512)S(6)} %eq.5), kind=kLoop, calls=%fused_computation.69 | loop fusion | flops 1966080 | bytes 5898242 | tf_op jit(solution)/shard_map/jit(_where)/select_n | solution.py:98
  151.6 3.0 maximum_select_fusion.1
  156.2 1.3 copy.224
  157.6 26.1 %all-reduce.2.cloned.1.call-done = bf16[3,2,640,640]{3,2,1,0:T(8,128)(2,1)} async-done(((bf16[3,2,640,640]{3,2,1,0:T(8,128)(2,1)}), bf16[3,2,640,640]{3,2,1,0:T(8,128)(2,1)}) %all-reduce.2.cloned.1.call-update) | async-done | bytes 4915216 | tf_op jit(solution)/shard_map/psum | solution.py:191
  183.7 6.8 %convert_element_type.74 = f32[3,2,640,640]{3,2,1,0:T(8,128)} convert(bf16[3,2,640,640]{3,2,1,0:T(8,128)(2,1)} %all-reduce.2.cloned.1.call-done) | non-fusion elementwise | flops 2457600 | bytes 14745600 | tf_op jit(solution)/shard_map/convert_element_type | solution.py:191
  190.6 1.1 slice.113
  191.7 1.3 maximum_select_fusion.refs_1_
  192.9 1.2 maximum_select_fusion.2.refs_4_
  194.2 18.4 %attend.1 = f32[2,256,1280]{2,1,0:T(8,128)} custom-call(bf16[2,256,1280]{2,1,0:T(8,128)(2,1)} %q_ref.1, bf16[2,256,1280]{2,1,0:T(8,128)(2,1)} %refs_0_, bf16[2,256,1280]{2,1,0:T(8,128)(2,1)} %maximum_select_fusion.refs_1_, bf16[2,256,1280]{2,1,0:T(8,128)(2,1)} %get-tuple-element.55.refs_2_, bf16[2,256,1280]{2,1,0:T(8,128)(2,1)} %refs_3_, ...), custom_call_target="tpu_custom_call" | custom-call | flops 2013265920 | bytes 26214400 | tf_op jit(solution)/shard_map/attend/pallas_call | solution.py:102
  212.6 7.2 %fusion = (f32[3,2,640]{2,1,0:T(2,128)S(1)}, f32[3,2,640]{2,1,0:T(2,128)S(1)}) fusion(bf16[3,2,640,640]{3,2,1,0:T(8,128)(2,1)} %all-gather.2.cloned.1.call-done, f32[3,2,640,640]{3,2,1,0:T(8,128)} %convert_element_type.74), kind=kLoop, calls=%fused_computation.2 | loop fusion | flops 14737920 | bytes 14776320 | tf_op jit(solution)/shard_map/reduce_sum | solution.py:189
  219.9 11.7 %fusion.100 = (bf16[3,2,640,640]{3,2,1,0:T(8,128)(2,1)}, f32[3,2,640,640]{3,2,1,0:T(8,128)}) fusion(f32[3,2,640]{2,1,0:T(2,128)S(1)} %rsqrt_multiply_fusion, f32[3,2,640,640]{3,2,1,0:T(8,128)} %convert_element_type.74, bf16[3,2,640,640]{3,2,1,0:T(8,128)(2,1)} %all-gather.2.cloned.1.call-done), kind=kLoop, calls=%fused_computation.126 | loop fusion | flops 9830400 | bytes 29506560 | tf_op jit(solution)/shard_map/convert_element_type | solution.py:208
  231.7 2.1 fusion.36
  233.8 2.1 fusion.33
  235.9 2.1 fusion.39
  240.6 2.8 pad_maximum_fusion.1
  244.1 2.1 fusion.37
  246.2 4.3 %fusion.21 = f32[2,640,256]{2,1,0:T(8,128)} fusion(bf16[3,2,640,640]{3,2,1,0:T(8,128)(2,1)} %get-tuple-element.45, bf16[256,2,640]{0,2,1:T(8,128)(2,1)S(1)} %bitcast.183, f32[256,2,640]{0,2,1:T(8,128)S(1)} %fusion.37), kind=kOutput, calls=%fused_computation.38 | convolution fusion | flops 840826880 | bytes 6553600 | tf_op jit(solution)/shard_map/nhf,hfd->nhd/dot_general | solution.py:38
  250.5 3.0 copy.213
  253.5 2.3 fusion.2
  255.8 2.4 copy.187
  258.2 4.7 %all-to-all-start = ((bf16[2,256,1280]{2,0,1:T(2,128)(2,1)}), bf16[2,256,1280]{2,0,1:T(2,128)(2,1)S(1)}, u32[]{:S(2)}, u32[]{:S(2)}) async-start(bf16[2,256,1280]{2,0,1:T(2,128)(2,1)} %copy.187), calls=%async_computation | async-start | bytes 2621440 | tf_op jit(solution)/shard_map/all_to_all | solution.py:222
  262.9 32.5 %all-to-all-done = bf16[2,256,1280]{2,0,1:T(2,128)(2,1)S(1)} async-done(((bf16[2,256,1280]{2,0,1:T(2,128)(2,1)}), bf16[2,256,1280]{2,0,1:T(2,128)(2,1)S(1)}, u32[]{:S(2)}, u32[]{:S(2)}) %all-to-all-start) | async-done | bytes 1310752 | tf_op jit(solution)/shard_map/all_to_all | solution.py:222
  295.3 1.4 multiply_reduce_fusion.1
  297.8 3.2 copy.188
  301.0 3.0 reshape.66
  304.1 1.4 multiply_convert_fusion
  305.5 2.2 multiply_reduce_fusion.2
  308.3 6.9 %sum_over.1 = f32[6,640]{1,0:T(8,128)} custom-call(f32[6,640]{1,0:T(8,128)} %reshape.65.x_ref), custom_call_target="tpu_custom_call" | custom-call | tf_op jit(solution)/shard_map/sum_over/pallas_call | solution.py:152
  316.0 1.9 fusion.79
  317.8 1.7 copy.191
  319.5 1.7 copy.190
  (67 shorter events, 15.1 us)
Async XLA Ops:
  7.2 2.4 copy-start.11
  7.2 2.5 copy-start.4
  7.2 45.6 %all-gather.2.cloned.1.call-start = ((), (), s32[]{:S(2)}) async-start(), calls=%async_computation.2 | async-start | bytes 5529600 | tf_op jit(solution)/shard_map/all_gather | solution.py:184
  9.5 174.1 %all-reduce.2.cloned.1.call-start = ((), (), s32[]{:S(2)}) async-start(), calls=%async_computation.3 | async-start | bytes 9830400 | tf_op jit(solution)/shard_map/psum | solution.py:191
  9.8 1.3 copy-start.5
  11.1 43.8 %copy-start.7 = (bf16[1,256,1280]{1,2,0:T(8,128)(2,1)}, bf16[1,256,1280]{1,2,0:T(8,128)(2,1)S(1)}, u32[]{:S(2)}) copy-start(bf16[1,256,1280]{1,2,0:T(8,128)(2,1)S(1)} %copy.223) | copy-start | bytes 1966084
  57.1 2.2 copy-start.2
  59.3 48.1 %collective-permute-start = (bf16[2,256,1280]{2,1,0:T(8,128)(2,1)S(1)}, bf16[2,256,1280]{2,1,0:T(8,128)(2,1)}, u32[]{:S(2)}, u32[]{:S(2)}) collective-permute-start(bf16[2,256,1280]{2,1,0:T(8,128)(2,1)S(1)} %copy-done.2), channel_id=1, source_target_pairs={{0,8},{4,12},{8,16},{12,20},{16,24},{20,28},{24,0},{28,4},{1,9},{5... | collective-permute-start | bytes 3932168 | tf_op jit(solution)/shard_map/ppermute | solution.py:21
  60.8 85.0 %collective-permute-start.1 = (bf16[2,256,1280]{2,1,0:T(8,128)(2,1)}, bf16[2,256,1280]{2,1,0:T(8,128)(2,1)}, u32[]{:S(2)}, u32[]{:S(2)}) collective-permute-start(bf16[2,256,1280]{2,1,0:T(8,128)(2,1)} %refs_3_), channel_id=1, source_target_pairs={{0,8},{4,12},{8,16},{12,20},{16,24},{20,28},{24,0},{28,4},{1,9},{5... | collective-permute-start | bytes 3932168 | tf_op jit(solution)/shard_map/ppermute | solution.py:21
  62.1 1.1 copy-start.8
  67.8 1.3 copy-start.1
  67.8 237.7 %reduce-scatter.2.cloned.1.call-start = ((), (), s32[]{:S(2)}) async-start(), calls=%async_computation.4 | async-start | bytes 5529600 | tf_op jit(solution)/shard_map/reduce_scatter | solution.py:210
  71.7 0.8 copy-start.9
  154.6 35.9 %collective-permute-start.2 = (bf16[2,256,1280]{2,1,0:T(8,128)(2,1)}, bf16[2,256,1280]{2,1,0:T(8,128)(2,1)S(1)}, u32[]{:S(2)}, u32[]{:S(2)}) collective-permute-start(bf16[2,256,1280]{2,1,0:T(8,128)(2,1)} %get-tuple-element.56), channel_id=1, source_target_pairs={{0,4},{4,0},{8,12},{12,8},{16,20},{20,16},{24,28},{28,24},{1,5},{5... | collective-permute-start | bytes 3932168 | tf_op jit(solution)/shard_map/ppermute | solution.py:199
  154.6 35.9 %collective-permute-start.3 = (bf16[2,256,1280]{2,1,0:T(8,128)(2,1)}, bf16[2,256,1280]{2,1,0:T(8,128)(2,1)}, u32[]{:S(2)}, u32[]{:S(2)}) collective-permute-start(bf16[2,256,1280]{2,1,0:T(8,128)(2,1)} %get-tuple-element.54), channel_id=1, source_target_pairs={{0,4},{4,0},{8,12},{12,8},{16,20},{20,16},{24,28},{28,24},{1,5},{5... | collective-permute-start | bytes 3932168 | tf_op jit(solution)/shard_map/ppermute | solution.py:199
  219.9 11.8 %copy-start.6 = (bf16[1,256,1280]{1,2,0:T(8,128)(2,1)S(1)}, bf16[1,256,1280]{1,2,0:T(8,128)(2,1)}, u32[]{:S(2)}) copy-start(bf16[1,256,1280]{1,2,0:T(8,128)(2,1)} %copy.225) | copy-start | bytes 1966084
  250.5 3.0 copy-start
  258.2 37.1 %all-to-all-start = ((bf16[2,256,1280]{2,0,1:T(2,128)(2,1)}), bf16[2,256,1280]{2,0,1:T(2,128)(2,1)S(1)}, u32[]{:S(2)}, u32[]{:S(2)}) async-start(bf16[2,256,1280]{2,0,1:T(2,128)(2,1)} %copy.187), calls=%async_computation | async-start | bytes 2621440 | tf_op jit(solution)/shard_map/all_to_all | solution.py:222
  301.0 3.1 copy-start.10
  305.5 10.5 %copy-start.3 = (bf16[3,2,80,640]{3,2,1,0:T(8,128)(2,1)S(1)}, bf16[3,2,80,640]{3,2,1,0:T(8,128)(2,1)}, u32[]{:S(2)}) copy-start(bf16[3,2,80,640]{3,2,1,0:T(8,128)(2,1)} %reduce-scatter.2.cloned.1.call-done) | copy-start | bytes 1843204
Sparse Core Ops, SparseCore 0:
  10.5 42.3 all-gather.1
  67.9 115.6 all-reduce.1
  243.5 55.4 reduce-scatter.1
where the time goes:
time: 330 us; the launch traced here: 328 us
  waiting for transfers between devices  161 us (49%)
  other arithmetic  51.3 us (16%)
  local copies, waits for them, and re-layouts  35.1 us (11%)
  matrix products  32.9 us (10%)
  Pallas kernels  25.3 us (8%)
  between operations  14.1 us (4%)
  starting transfers between devices  8.11 us (2%)
    ppermute x2, waiting for transfers between devices, shift(): lax.ppermute(x, axis, [(i, (i + by) % length) for i in range(length)])  61.9 us
    all_gather x1, waiting for transfers between devices, local(): wb = lax.all_gather(shard.astype(jnp.bfloat16), 'aa', axis=2, tiled=True)  40.4 us
    all_to_all x1, waiting for transfers between devices, local(): lax.all_to_all(combined, 'ba', split_axis=1, concat_axis=2, tiled=True)  32.5 us
    psum x1, waiting for transfers between devices, local(): grads = lax.psum(gp, 'aa').astype(jnp.float32)  26.1 us
    pallas_call x1, Pallas kernels, attend(): pl.pallas_call(functools.partial(attend_kernel, rows, groups), grid=(stre...  18.4 us
    dot_general x8, matrix products, project(): return jnp.einsum('nhd,hfd->nhf', x, w, preferred_element_type=jnp.float32)  18.4 us
    unnamed x35, local copies, waits for them, and re-layouts  11.9 us
    convert_element_type x1, other arithmetic, local(): ub = updated.astype(jnp.bfloat16)  11.7 us
  transfers between devices with their start and end apart: 8, of which 5 were waited for; matrix products, arithmetic and copies ran while one was open for 20% of the time, Pallas kernels for 0%

commit v1 on v0

--- a/solution.py
+++ b/solution.py
@@ -227,11 +227,437 @@
     return (mixed, jnp.transpose(weights, back), jnp.transpose(moment, back))
 
 
+class Comm:
+    def __init__(self, send, recv):
+        self.send, self.recv, self.used = send, recv, 0
+        self.open = []
+
+    def slots(self, count):
+        first = self.used
+        self.used += count
+        return first
+
+    def make(self, slot, src, dst, peer):
+        return pltpu.make_async_remote_copy(
+            src_ref=src,
+            dst_ref=dst,
+            send_sem=self.send.at[slot],
+            recv_sem=self.recv.at[slot],
+            device_id=peer,
+            device_id_type=pl.DeviceIdType.MESH,
+        )
+
+
+NT = (((1,), (1,)), ((), ()))
+TN = (((0,), (0,)), ((), ()))
+NN = (((1,), (0,)), ((), ()))
+
+
+def mm(a, b, dims):
+    return lax.dot_general(a, b, dims, preferred_element_type=jnp.float32)
+
+
+def block_kernel(
+    n,
+    parts,
+    fq,
+    fk,
+    fv,
+    rate,
+    aq,
+    ak,
+    av,
+    wb,
+    gain,
+    mixed,
+    weights,
+    moment,
+    gp,
+    pair,
+    sums,
+    ring,
+    full,
+    far,
+    near,
+    acc,
+    comb,
+    land,
+    target,
+    sq,
+    sqland,
+    send,
+    recv,
+):
+    me = lax.axis_index("aa")
+    mine = lax.axis_index("ba")
+    group, core = me // 2, lax.rem(me, 2)
+    teams = n // 2
+    heads = wb.shape[2]
+    r, depth = wb.shape[3], wb.shape[4]
+    stretches, rows, width = fq.shape
+    partner = {"aa": group * 2 + 1 - core}
+    comm = Comm(send, recv)
+
+    def peer(step):
+        return lax.rem(group + step, teams)
+
+    def source(step):
+        return lax.rem(group + teams - step, teams)
+
+    def same(g):
+        return {"aa": g * 2 + core}
+
+    barrier = pltpu.get_barrier_semaphore()
+    for step in range(1, n):
+        pl.semaphore_signal(
+            barrier,
+            inc=1,
+            device_id={"aa": lax.rem(me + step, n)},
+            device_id_type=pl.DeviceIdType.MESH,
+        )
+    for step in range(1, parts):
+        pl.semaphore_signal(
+            barrier,
+            inc=1,
+            device_id={"ba": lax.rem(mine + step, parts)},
+            device_id_type=pl.DeviceIdType.MESH,
+        )
+    pl.semaphore_wait(barrier, n + parts - 2)
+
+    pending = []
+    halo_first = comm.slots(4 * stretches)
+    held = (ak, av)
+
+    def halo(t, s):
+        slot = halo_first + t * stretches + s
+        copy = comm.make(slot, held[t].at[s], far.at[t, s], same(peer(1)))
+        copy.start()
+        pending.append(copy)
+        return copy
+
+    def swap(t, s):
+        slot = halo_first + 2 * stretches + t * stretches + s
+
+        @pl.when(core == 0)
+        def _():
+            comm.make(slot, held[t].at[s], near.at[t, s], partner).start()
+
+        @pl.when(core == 1)
+        def _():
+            comm.make(slot, far.at[t, s], near.at[t, s], partner).start()
+
+        copy = comm.make(slot, held[t].at[s], near.at[t, s], partner)
+        pending.append(copy)
+        return copy
+
+    def whole(ref, m, h):
+        return ref[:, m, h].reshape(n * r, depth)
+
+    def grads(ref, s):
+        @pl.loop(0, heads)
+        def _(h):
+            cols = pl.ds(pl.multiple_of(h * depth, 128), depth)
+            k = fk[s, :, cols]
+            v = fv[s, :, cols]
+            gate_in = mm(k, whole(ref, 0, h), NT)
+            up_in = mm(k, whole(ref, 1, h), NT)
+            back_in = mm(v, whole(ref, 2, h), NT)
+            act, slope = activation(gate_in)
+            xs = (
+                (rate[s, h, 0] * (-back_in * up_in * slope)).astype(jnp.bfloat16),
+                (rate[s, h, 1] * (-back_in * act)).astype(jnp.bfloat16),
+                (rate[s, h, 2] * -(act * up_in)).astype(jnp.bfloat16),
+            )
+            for m in range(3):
+                part = mm(xs[m], v if m == 2 else k, TN).astype(jnp.bfloat16)
+                gp[:, :, m, h] = part.reshape(teams, 2, r, depth)
+
+    def forward(ref, s):
+        @pl.loop(0, heads)
+        def _(h):
+            cols = pl.ds(pl.multiple_of(h * depth, 128), depth)
+            q = fq[s, :, cols]
+            act, _ = activation(mm(q, whole(ref, 0, h), NT))
+            hidden = (act * mm(q, whole(ref, 1, h), NT)).astype(jnp.bfloat16)
+            acc[s, :, cols] = mm(hidden, whole(ref, 2, h), NN)
+
+    def attention(s):
+        base = s * (rows * n) + me * rows
+        places = [s] + [jnp.where(me < b, max(s - 1, 0), s) for b in (1, 2)]
+        row = lax.broadcasted_iota(jnp.int32, (rows, rows), 0)
+        col = lax.broadcasted_iota(jnp.int32, (rows, rows), 1)
+        oks = []
+        for back in range(3):
+            gap = row - col + back * rows
+            oks.append((gap >= 0) & (gap < WINDOW) & (col >= back * rows - base))
+
+        @pl.loop(0, width // AD)
+        def _(h):
+            cols = pl.ds(pl.multiple_of(h * AD, AD), AD)
+            keys = [ak[s, :, cols], near[0, places[1], :, cols], far[0, places[2], :, cols]]
+            values = [av[s, :, cols], near[1, places[1], :, cols], far[1, places[2], :, cols]]
+            q = aq[s, :, cols]
+            scores = [
+                jnp.where(ok, mm(q, k, NT) / math.sqrt(AD), -1e30) for ok, k in zip(oks, keys)
+            ]
+            top = functools.reduce(
+                jnp.maximum, [jnp.max(x, -1, keepdims=True) for x in scores]
+            )
+            total, out = 0.0, 0.0
+            for x, v in zip(scores, values):
+                p = jnp.exp(x - top)
+                total = total + jnp.sum(p, -1, keepdims=True)
+                out = out + mm(p.astype(jnp.bfloat16), v, NN)
+            comb[s, :, cols] = (acc[s, :, cols] + out / total).astype(jnp.bfloat16)
+
+    def pair_send(phase):
+        first = comm.slots(teams)
+        copies = []
+        for g in range(teams):
+            copy = comm.make(first + g, gp.at[g, 1 - core], pair.at[phase, g], partner)
+            copy.start()
+            copies.append(copy)
+        return copies
+
+    def ring_send(phase, copies):
+        first = comm.slots(teams)
+        for copy in copies:
+            copy.wait()
+        out = []
+        for step in range(1, teams):
+            g = peer(step)
+
+            @pl.loop(0, heads)
+            def _(h):
+                for m in range(3):
+                    sums[g, m, h] = (
+                        gp[g, core, m, h].astype(jnp.float32)
+                        + pair[phase, g, m, h].astype(jnp.float32)
+                    ).astype(jnp.bfloat16)
+
+        for step in range(1, teams):
+            g = peer(step)
+            copy = comm.make(first + step, sums.at[g], ring.at[phase, step], same(g))
+            copy.start()
+            out.append(copy)
+        return out
+
+    def total_of(phase, m, h):
+        total = gp[group, core, m, h].astype(jnp.float32) + pair[phase, group, m, h].astype(
+            jnp.float32
+        )
+        for step in range(1, teams):
+            total = total + ring[phase, step, m, h].astype(jnp.float32)
+        return total
+
+    def exchange(s):
+        first = comm.slots(parts)
+        chunk = rows // parts
+        copies = []
+        for step in range(1, parts):
+            z = lax.rem(mine + step, parts)
+            take = pl.ds(pl.multiple_of(z * chunk, chunk), chunk)
+            copy = comm.make(first + step, comb.at[s, take], land.at[s, step], {"ba": z})
+            copy.start()
+            copies.append(copy)
+        return copies
+
+    def finish(s, copies):
+        chunk = rows // parts
+        take = pl.ds(pl.multiple_of(mine * chunk, chunk), chunk)
+        land[s, 0] = comb[s, take]
+        for copy in copies:
+            copy.wait()
+        squares = 0.0
+        for step in range(parts):
+            x = land[s, step].astype(jnp.float32)
+            squares = squares + jnp.sum(x * x, -1, keepdims=True)
+        scale = lax.rsqrt(squares / (parts * width) + EPS)
+        for step in range(parts):
+            z = lax.rem(mine + parts - step, parts)
+            cols = pl.ds(pl.multiple_of(z * width, 128), width)
+            x = land[s, step].astype(jnp.float32)
+            mixed[s, :, cols] = (x * scale * gain[:, cols]).astype(jnp.bfloat16)
+
+    keys0 = halo(0, 0)
+    grads(wb, 0)
+    copies = pair_send(0)
+    forward(wb, 0)
+    copies = ring_send(0, copies)
+    values0 = halo(1, 0)
+    for copy in copies:
+        copy.wait()
+
+    @pl.loop(0, heads)
+    def _(h):
+        for m in range(3):
+            full[me, m, h] = total_of(0, m, h).astype(jnp.bfloat16)
+
+    first = comm.slots(2 * teams)
+    gathers = []
+    for step in range(1, teams):
+        copy = comm.make(first + step, full.at[me], full.at[me], same(peer(step)))
+        copy.start()
+        gathers.append(copy)
+    near_copy = comm.make(first + teams, full.at[me], full.at[me], partner)
+    near_copy.start()
+    later = [halo(t, 1) for t in range(2)]
+    keys0.wait_recv()
+    values0.wait_recv()
+    swaps = [swap(t, 0) for t in range(2)]
+    for copy in swaps:
+        copy.wait_recv()
+    attention(0)
+    mixing0 = exchange(0)
+    forwards = []
+    for step in range(1, teams):
+        gathers[step - 1].wait_recv()
+        block = source(step) * 2 + core
+        copy = comm.make(first + teams + step, full.at[block], full.at[block], partner)
+        copy.start()
+        forwards.append(copy)
+    near_copy.wait()
+    for copy in gathers:
+        copy.wait_send()
+    for copy in forwards:
+        copy.wait()
+
+    @pl.loop(0, heads)
+    def _(h):
+        for m in range(3):
+            before, after = 0.0, 0.0
+            for j in range(n):
+                w = wb[j, m, h].astype(jnp.float32)
+                t = w - full[j, m, h].astype(jnp.float32)
+                before = before + jnp.sum(w * w, 0, keepdims=True)
+                after = after + jnp.sum(t * t, 0, keepdims=True)
+            goal = jnp.sqrt(before + EPS)
+            target[m, h] = goal
+            ratio = goal / jnp.sqrt(after + EPS)
+            past = full[me, m, h].astype(jnp.float32)
+            moment[m, h] = past
+            weights[m, h] = (wb[me, m, h].astype(jnp.float32) - past) * ratio
+            for j in range(n):
+                w = wb[j, m, h].astype(jnp.float32)
+                t = w - full[j, m, h].astype(jnp.float32)
+                full[j, m, h] = (t * ratio).astype(jnp.bfloat16)
+
+    grads(full, 1)
+    copies = pair_send(1)
+    forward(full, 1)
+    copies = ring_send(1, copies)
+    for copy in later:
+        copy.wait_recv()
+    swaps = [swap(t, 1) for t in range(2)]
+    for copy in swaps:
+        copy.wait_recv()
+    attention(1)
+    mixing1 = exchange(1)
+    finish(0, mixing0)
+    for copy in copies:
+        copy.wait()
+
+    @pl.loop(0, heads)
+    def _(h):
+        for m in range(3):
+            momentum = BETA * moment[m, h] + total_of(1, m, h)
+            moment[m, h] = momentum
+            trial = weights[m, h] - momentum
+            weights[m, h] = trial
+            sq[m, h] = jnp.sum(trial * trial, 0, keepdims=True)
+
+    first = comm.slots(n)
+    copies = []
+    for step in range(1, n):
+        copy = comm.make(
+            first + step, sq, sqland.at[step], {"aa": lax.rem(me + step, n)}
+        )
+        copy.start()
+        copies.append(copy)
+    finish(1, mixing1)
+    for copy in copies:
+        copy.wait()
+
+    @pl.loop(0, heads)
+    def _(h):
+        for m in range(3):
+            squares = sq[m, h]
+            for step in range(1, n):
+                squares = squares + sqland[step, m, h]
+            weights[m, h] = weights[m, h] * (target[m, h] / jnp.sqrt(squares + EPS))
+
+    for copy in pending:
+        copy.wait_send()
+
+
+def run_blocks(fq, fk, fv, rates, aq, ak, av, wb, gain):
+    n, parts = lax.axis_size("aa"), lax.axis_size("ba")
+    stretches, rows, width = fq.shape
+    heads, r, depth = wb.shape[2:]
+    teams = n // 2
+    vmem = pl.BlockSpec(memory_space=pltpu.VMEM)
+    shard = (3, heads, r, depth)
+    small = (3, heads, 1, depth)
+    bf, f32 = jnp.bfloat16, jnp.float32
+    slots = 4 * stretches + 2 * (2 * teams) + 2 * teams + 2 * parts + n
+    return pl.pallas_call(
+        functools.partial(block_kernel, n, parts),
+        in_specs=[vmem] * 9,
+        out_specs=(vmem,) * 3,
+        out_shape=(
+            jax.ShapeDtypeStruct((stretches, rows // parts, width * parts), bf),
+            jax.ShapeDtypeStruct(shard, f32),
+            jax.ShapeDtypeStruct(shard, f32),
+        ),
+        scratch_shapes=[
+            pltpu.VMEM((teams, 2) + shard, bf),
+            pltpu.VMEM((2, teams) + shard, bf),
+            pltpu.VMEM((teams,) + shard, bf),
+            pltpu.VMEM((2, teams) + shard, bf),
+            pltpu.VMEM((n,) + shard, bf),
+            pltpu.VMEM((2, stretches, rows, width), bf),
+            pltpu.VMEM((2, stretches, rows, width), bf),
+            pltpu.VMEM((stretches, rows, width), f32),
+            pltpu.VMEM((stretches, rows, width), bf),
+            pltpu.VMEM((stretches, parts, rows // parts, width), bf),
+            pltpu.VMEM(small, f32),
+            pltpu.VMEM(small, f32),
+            pltpu.VMEM((n,) + small, f32),
+            pltpu.SemaphoreType.DMA((slots,)),
+            pltpu.SemaphoreType.DMA((slots,)),
+        ],
+        compiler_params=pltpu.CompilerParams(
+            collective_id=2, has_side_effects=True, vmem_limit_bytes=67043328
+        ),
+        name="blocks",
+    )(fq, fk, fv, rates, aq, ak, av, wb, gain)
+
+
+def local_blocks(fq, fk, fv, rates, aq, ak, av, fast_weights, gain):
+    stretches, rows, _ = fq.shape
+    heads = fast_weights.shape[2]
+    shard = jnp.transpose(fast_weights, (1, 2, 0, 3)).astype(jnp.bfloat16)
+    wb = lax.all_gather(shard, "aa", axis=0)
+    rate = jnp.transpose(rates.reshape(stretches, rows, heads, 3), (0, 2, 3, 1))[..., None]
+    mixed, weights, moment = run_blocks(fq, fk, fv, rate, aq, ak, av, wb, gain[None])
+    back = (2, 0, 1, 3)
+    return (mixed, jnp.transpose(weights, back), jnp.transpose(moment, back))
+
+
+def pick(*args):
+    stretches, rows, _ = args[0].shape
+    r, _, _, depth = args[7].shape
+    n, parts = lax.axis_size("aa"), lax.axis_size("ba")
+    fits = r % 16 == 0 and n % 2 == 0 and n > 2 and depth % AD == 0 and stretches == 2
+    fits = fits and 2 * rows == WINDOW and rows % (16 * parts) == 0
+    return (local_blocks if fits else local)(*args)
+
+
 def solution(mesh):
     token = P(None, "aa", "ba")
     hidden = P("aa", None, "ba", None)
     return jax.shard_map(
-        local,
+        pick,
         mesh=mesh,
         in_specs=(token,) * 7 + (hidden, P()),
         out_specs=(P(None, ("aa", "ba"), None), hidden, hidden),

time: 330 us -> 226 us (0.68)
  Pallas kernels: 25.3 us -> 153 us
  waiting for transfers between devices: 161 us -> 43.3 us
  other arithmetic: 51.3 us -> 2.53 us
  matrix products: 32.9 us -> 0 us
  local copies, waits for them, and re-layouts: 35.1 us -> 13.1 us
  starting transfers between devices: 8.11 us -> 0.04 us
    pallas_call x2 -> x1, Pallas kernels: 25.3 us -> 153 us  [run_blocks(): pl.pallas_call(functools.partial(block_kernel, n, parts), in_specs=[vmem]...]
    ppermute x4 -> x0, waiting for transfers between devices: 61.9 us -> none  [the longest x2 61.9 us: shift(): lax.ppermute(x, axis, [(i, (i + by) % length) for i in range(length)])]
    dot_general x16 -> x0, matrix products: 32.9 us -> none  [the longest x8 18.4 us: project(): return jnp.einsum('nhd,hfd->nhf', x, w, preferred_element_type=jnp.float32)]
    all_to_all x1 -> x0, waiting for transfers between devices: 32.5 us -> none  [local(): lax.all_to_all(combined, 'ba', split_axis=1, concat_axis=2, tiled=True)]
    psum x1 -> x0, waiting for transfers between devices: 26.1 us -> none  [local(): grads = lax.psum(gp, 'aa').astype(jnp.float32)]
    convert_element_type x5 -> x1, other arithmetic: 23.2 us -> 2.53 us  [local_blocks(): shard = jnp.transpose(fast_weights, (1, 2, 0, 3)).astype(jnp.bfloat16)]
    reduce_sum x4 -> x0, other arithmetic: 10.9 us -> none  [the longest x1 7.25 us: local(): target = jnp.sqrt(jnp.sum(full * full, 2, keepdims=True) + EPS)]
    select_n x4 -> x0, other arithmetic: 8.98 us -> none  [moved(): return jnp.where(index < back, jnp.concatenate([x[:1], x[:-1]], 0), x)]
  transfers between devices with their start and end apart: 8 -> 1, of which waited for: 5 -> 1; matrix products, arithmetic and copies ran while one was open for 20% -> 1% of each run, Pallas kernels for 0% -> 0%
where the time goes in v1:
time: 226 us
  Pallas kernels  153 us (68%)
  waiting for transfers between devices  43.3 us (19%)
  between operations  14.1 us (6%)
  local copies, waits for them, and re-layouts  13.1 us (6%)
  other arithmetic  2.53 us (1%)
    pallas_call x1, Pallas kernels, run_blocks(): pl.pallas_call(functools.partial(block_kernel, n, parts), in_specs=[vmem]...  153 us
    all_gather x1, waiting for transfers between devices, local_blocks(): wb = lax.all_gather(shard, 'aa', axis=0)  43.3 us
    unnamed x9, local copies, waits for them, and re-layouts  5.78 us
    all_gather x1, local copies, waits for them, and re-layouts, local_blocks(): wb = lax.all_gather(shard, 'aa', axis=0)  5.66 us
  transfers between devices with their start and end apart: 1, of which 1 were waited for; matrix products, arithmetic and copies ran while one was open for 1% of the time, Pallas kernels for 0%

profile of v1, /device:TPU:0, one launch (start us, length us, event | category | flops | bytes accessed | tf_op | source)
XLA Modules:
  0.0 226.0 jit_solution(4830460928334941983)
XLA Ops:
  7.2 0.0 copy-start.2
  7.2 0.0 all-gather.3.cloned.1.call-start
  7.2 2.5 %convert_bitcast_fusion = bf16[3,2,80,640]{3,1,0,2:T(2,128)(2,1)} fusion(f32[80,3,2,640]{3,2,1,0:T(2,128)} %param.16), kind=kLoop, calls=%fused_computation | loop fusion | flops 307200 | bytes 1843200 | tf_op jit(solution)/shard_map/convert_element_type | solution.py:639
  9.8 0.0 all-gather.3.cloned.1.call-update
  9.8 0.0 copy-done.2
  9.8 1.7 copy.18.rate
  11.5 43.3 %all-gather.3.cloned.1.call-done = bf16[24,2,80,640]{3,1,0,2:T(2,128)(2,1)} async-done(((bf16[3,2,80,640]{3,1,0,2:T(2,128)(2,1)}), bf16[24,2,80,640]{3,1,0,2:T(2,128)(2,1)}) %all-gather.3.cloned.1.call-update) | async-done | bytes 4915216 | tf_op jit(solution)/shard_map/all_gather | solution.py:640
  54.7 5.7 %copy.17 = bf16[24,2,80,640]{3,2,1,0:T(8,128)(2,1)} copy(bf16[24,2,80,640]{3,1,0,2:T(2,128)(2,1)} %all-gather.3.cloned.1.call-done) | data formatting | bytes 9830400 | tf_op jit(solution)/shard_map/all_gather | solution.py:640
  60.4 153.0 %blocks.1 = (bf16[2,64,5120]{2,1,0:T(8,128)(2,1)}, f32[3,2,80,640]{3,2,1,0:T(8,128)}, f32[3,2,80,640]{3,2,1,0:T(8,128)}) custom-call(bf16[2,256,1280]{2,1,0:T(8,128)(2,1)} %fq.1, bf16[2,256,1280]{2,1,0:T(8,128)(2,1)} %fk.1, bf16[2,256,1280]{2,1,0:T(8,128)(2,1)} %fv.1, f32[2,2,3,256,1]{4,3,2,1,0:T(8,128)} %copy.18.rate, bf16[2,256,1280]{2,1,0:T(8,128)(2,1)} %aq.1, ...), custom_call_target="tpu_custom_call" | custom-call | tf_op jit(solution)/shard_map/blocks/pallas_call | solution.py:603
  213.4 0.0 copy-start.1
  213.4 3.0 %copy.19 = f32[80,3,2,640]{3,2,1,0:T(2,128)} copy(f32[80,3,2,640]{3,0,2,1:T(8,128)} %bitcast.13) | data formatting | bytes 2457600
  216.4 0.0 copy-start
  216.4 0.0 copy-done.1
  216.4 1.7 copy.20
  218.1 0.0 copy-done
  218.1 1.1 copy.24
Async XLA Ops:
  7.2 2.6 %copy-start.2 = (f32[2,256,6]{1,0,2:T(2,128)S(1)}, f32[2,256,6]{1,0,2:T(2,128)}, u32[]{:S(2)}) copy-start(f32[2,256,6]{1,0,2:T(2,128)} %param.12) | copy-start | bytes 36868
  7.2 47.5 %all-gather.3.cloned.1.call-start = ((), (), s32[]{:S(2)}) async-start(), calls=%async_computation | async-start | bytes 5529600 | tf_op jit(solution)/shard_map/all_gather | solution.py:640
  213.4 3.1 %copy-start.1 = (f32[3,2,80,640]{3,2,1,0:T(8,128)S(1)}, f32[3,2,80,640]{3,2,1,0:T(8,128)}, u32[]{:S(2)}) copy-start(f32[3,2,80,640]{3,2,1,0:T(8,128)} %get-tuple-element.8) | copy-start | bytes 3686404
  216.4 1.7 copy-start
Sparse Core Ops, SparseCore 0:
  10.4 44.2 all-gather.2

commit v2 on v1

--- a/solution.py
+++ b/solution.py
@@ -230,19 +230,18 @@
 class Comm:
     def __init__(self, send, recv):
         self.send, self.recv, self.used = send, recv, 0
-        self.open = []
 
     def slots(self, count):
         first = self.used
         self.used += count
         return first
 
-    def make(self, slot, src, dst, peer):
+    def make(self, slot, src, dst, peer, lands=None):
         return pltpu.make_async_remote_copy(
             src_ref=src,
             dst_ref=dst,
             send_sem=self.send.at[slot],
-            recv_sem=self.recv.at[slot],
+            recv_sem=self.recv.at[slot if lands is None else lands],
             device_id=peer,
             device_id_type=pl.DeviceIdType.MESH,
         )
@@ -251,10 +250,6 @@
 NT = (((1,), (1,)), ((), ()))
 TN = (((0,), (0,)), ((), ()))
 NN = (((1,), (0,)), ((), ()))
-
-
-def mm(a, b, dims):
-    return lax.dot_general(a, b, dims, preferred_element_type=jnp.float32)
 
 
 def block_kernel(
@@ -267,18 +262,22 @@
     aq,
     ak,
     av,
-    wb,
+    shard,
     gain,
     mixed,
     weights,
     moment,
     gp,
     pair,
-    sums,
-    ring,
+    first_sums,
+    second_sums,
+    first_land,
+    second_land,
+    start,
     full,
     far,
     near,
+    relay,
     acc,
     comb,
     land,
@@ -292,20 +291,18 @@
     mine = lax.axis_index("ba")
     group, core = me // 2, lax.rem(me, 2)
     teams = n // 2
-    heads = wb.shape[2]
-    r, depth = wb.shape[3], wb.shape[4]
+    heads, _, r, depth = shard.shape
     stretches, rows, width = fq.shape
+    row_at, col_at = group // 2, lax.rem(group, 2)
+    beside = row_at * 2 + 1 - col_at
+    above = (1 - row_at) * 2 + col_at
+    across = (1 - row_at) * 2 + 1 - col_at
     partner = {"aa": group * 2 + 1 - core}
+    to_x = {"aa": beside * 2 + core}
+    to_y = {"aa": above * 2 + core}
     comm = Comm(send, recv)
-
-    def peer(step):
-        return lax.rem(group + step, teams)
-
-    def source(step):
-        return lax.rem(group + teams - step, teams)
-
-    def same(g):
-        return {"aa": g * 2 + core}
+    bf, f32 = jnp.bfloat16, jnp.float32
+    via_y, via_x = pl.ds(0, 2), pl.ds(2, 1)
 
     barrier = pltpu.get_barrier_semaphore()
     for step in range(1, n):
@@ -324,53 +321,128 @@
         )
     pl.semaphore_wait(barrier, n + parts - 2)
 
-    pending = []
-    halo_first = comm.slots(4 * stretches)
     held = (ak, av)
-
-    def halo(t, s):
-        slot = halo_first + t * stretches + s
-        copy = comm.make(slot, held[t].at[s], far.at[t, s], same(peer(1)))
-        copy.start()
-        pending.append(copy)
-        return copy
-
-    def swap(t, s):
-        slot = halo_first + 2 * stretches + t * stretches + s
-
-        @pl.when(core == 0)
+    final = comm.slots(2 * stretches)
+    relays = comm.slots(stretches)
+    swaps = comm.slots(2 * stretches)
+
+    def halo_copy(t, s, direct):
+        slot = final + t * stretches + s
+        if direct:
+            return comm.make(slot, held[t].at[s], far.at[t, s], to_x)
+        return comm.make(slot, held[t].at[s], relay.at[s], (to_x, to_y)[t], relays + s)
+
+    def halo(s):
+        for t in range(2):
+
+            @pl.when(col_at == 0)
+            def _():
+                halo_copy(t, s, True).start()
+
+            @pl.when(col_at == 1)
+            def _():
+                halo_copy(t, s, False).start()
+
+    def halo_relay(s):
+        halo_copy(0, s, False).wait_recv()
+
+        @pl.when(col_at == 0)
         def _():
-            comm.make(slot, held[t].at[s], near.at[t, s], partner).start()
-
-        @pl.when(core == 1)
+            comm.make(relays + s, relay.at[s], far.at[0, s], to_y, final + s).start()
+
+        @pl.when(col_at == 1)
         def _():
-            comm.make(slot, far.at[t, s], near.at[t, s], partner).start()
-
-        copy = comm.make(slot, held[t].at[s], near.at[t, s], partner)
-        pending.append(copy)
-        return copy
+            comm.make(
+                relays + s, relay.at[s], far.at[1, s], to_x, final + stretches + s
+            ).start()
+
+    def halo_swap(s):
+        copies = []
+        for t in range(2):
+            slot = swaps + t * stretches + s
+            halo_copy(t, s, True).wait_recv()
+
+            @pl.when(core == 0)
+            def _():
+                comm.make(slot, held[t].at[s], near.at[t, s], partner).start()
+
+            @pl.when(core == 1)
+            def _():
+                comm.make(slot, far.at[t, s], near.at[t, s], partner).start()
+
+            copies.append(comm.make(slot, held[t].at[s], near.at[t, s], partner))
+        for copy in copies:
+            copy.wait()
+
+    def halo_sent(s):
+        for t in range(2):
+            halo_copy(t, s, True).wait_send()
+        comm.make(relays + s, relay.at[s], far.at[0, s], to_y).wait_send()
+
+    def gather_start(buf, h, src):
+        first = comm.slots(9)
+        own = buf.at[h, me]
+        copies = [
+            comm.make(first, src, own, to_x),
+            comm.make(first + 1, src, own, to_y),
+            comm.make(first + 4, src, own, partner),
+        ]
+        for copy in copies:
+            copy.start()
+        return first, copies
+
+    def gather_relay(buf, h, state):
+        first, copies = state
+        for k, (block, peer, ms) in enumerate(((beside, to_y, via_y), (above, to_x, via_x))):
+            copies[k].wait_recv()
+            at = block * 2 + core
+            piece = buf.at[h, at, ms]
+            onward = comm.make(first + 2 + k, piece, piece, peer)
+            onward.start()
+            twin = comm.make(first + 5 + k, buf.at[h, at], buf.at[h, at], partner)
+            twin.start()
+            copies += [onward, twin]
+
+    def gather_end(buf, h, state):
+        first, copies = state
+        at = across * 2 + core
+        for k, ms in enumerate((via_y, via_x)):
+            piece = buf.at[h, at, ms]
+            comm.make(first + 2 + k, piece, piece, partner).wait_recv()
+            twin = comm.make(first + 7 + k, piece, piece, partner)
+            twin.start()
+            copies.append(twin)
+        copies[2].wait_recv()
+        copies[4].wait_recv()
+        copies[6].wait_recv()
+        copies[7].wait_recv()
+        copies[8].wait_recv()
+        for copy in copies:
+            copy.wait_send()
+
+    def mm(a, b, dims):
+        return lax.dot_general(a, b, dims, preferred_element_type=f32)
 
     def whole(ref, m, h):
-        return ref[:, m, h].reshape(n * r, depth)
-
-    def grads(ref, s):
-        @pl.loop(0, heads)
-        def _(h):
-            cols = pl.ds(pl.multiple_of(h * depth, 128), depth)
-            k = fk[s, :, cols]
-            v = fv[s, :, cols]
-            gate_in = mm(k, whole(ref, 0, h), NT)
-            up_in = mm(k, whole(ref, 1, h), NT)
-            back_in = mm(v, whole(ref, 2, h), NT)
-            act, slope = activation(gate_in)
-            xs = (
-                (rate[s, h, 0] * (-back_in * up_in * slope)).astype(jnp.bfloat16),
-                (rate[s, h, 1] * (-back_in * act)).astype(jnp.bfloat16),
-                (rate[s, h, 2] * -(act * up_in)).astype(jnp.bfloat16),
-            )
-            for m in range(3):
-                part = mm(xs[m], v if m == 2 else k, TN).astype(jnp.bfloat16)
-                gp[:, :, m, h] = part.reshape(teams, 2, r, depth)
+        return ref[h, :, m].reshape(n * r, depth)
+
+    def grads(ref, s, h):
+        cols = pl.ds(h * depth, depth)
+        k = fk[s, :, cols]
+        v = fv[s, :, cols]
+        gate_in = mm(k, whole(ref, 0, h), NT)
+        up_in = mm(k, whole(ref, 1, h), NT)
+        back_in = mm(v, whole(ref, 2, h), NT)
+        act, slope = activation(gate_in)
+        xs = (
+            (rate[s, h, 0] * (-back_in * up_in * slope)).astype(bf),
+            (rate[s, h, 1] * (-back_in * act)).astype(bf),
+            (rate[s, h, 2] * -(act * up_in)).astype(bf),
+        )
+        for m in range(3):
+            part = mm(xs[m], v if m == 2 else k, TN).astype(bf).reshape(teams, 2, r, depth)
+            for c in range(2):
+                gp[h, c, :, m] = part[:, c]
 
     def forward(ref, s):
         @pl.loop(0, heads)
@@ -378,7 +450,7 @@
             cols = pl.ds(pl.multiple_of(h * depth, 128), depth)
             q = fq[s, :, cols]
             act, _ = activation(mm(q, whole(ref, 0, h), NT))
-            hidden = (act * mm(q, whole(ref, 1, h), NT)).astype(jnp.bfloat16)
+            hidden = (act * mm(q, whole(ref, 1, h), NT)).astype(bf)
             acc[s, :, cols] = mm(hidden, whole(ref, 2, h), NN)
 
     def attention(s):
@@ -407,48 +479,72 @@
             for x, v in zip(scores, values):
                 p = jnp.exp(x - top)
                 total = total + jnp.sum(p, -1, keepdims=True)
-                out = out + mm(p.astype(jnp.bfloat16), v, NN)
-            comb[s, :, cols] = (acc[s, :, cols] + out / total).astype(jnp.bfloat16)
-
-    def pair_send(phase):
-        first = comm.slots(teams)
-        copies = []
-        for g in range(teams):
-            copy = comm.make(first + g, gp.at[g, 1 - core], pair.at[phase, g], partner)
+                out = out + mm(p.astype(bf), v, NN)
+            comb[s, :, cols] = (acc[s, :, cols] + out / total).astype(bf)
+
+    def pair_send(phase, h):
+        slot = comm.slots(1)
+        copy = comm.make(slot, gp.at[h, 1 - core], pair.at[phase, h], partner)
+        copy.start()
+        return copy
+
+    def both(phase, h, g, m):
+        return gp[h, core, g, m].astype(f32) + pair[phase, h, g, m].astype(f32)
+
+    def reduce_first(phase, h, copy):
+        copy.wait()
+        for k, g in enumerate((above, across)):
+            for m in range(2):
+                first_sums[h, k, m] = both(phase, h, g, m).astype(bf)
+        for k, g in enumerate((beside, across)):
+            first_sums[h, 2 + k, 0] = both(phase, h, g, 2).astype(bf)
+        slot = comm.slots(3)
+        copies = [
+            comm.make(
+                slot,
+                first_sums.at[h, pl.ds(0, 2)],
+                first_land.at[phase, h, pl.ds(0, 2)],
+                to_y,
+            )
+        ]
+        for k in range(2, 4):
+            copies.append(
+                comm.make(
+                    slot + k - 1,
+                    first_sums.at[h, k, pl.ds(0, 1)],
+                    first_land.at[phase, h, k, pl.ds(0, 1)],
+                    to_x,
+                )
+            )
+        for copy in copies:
             copy.start()
-            copies.append(copy)
         return copies
 
-    def ring_send(phase, copies):
-        first = comm.slots(teams)
+    def reduce_second(phase, h, copies):
         for copy in copies:
             copy.wait()
+        for m in range(2):
+            second_sums[h, m] = (
+                both(phase, h, beside, m) + first_land[phase, h, 1, m].astype(f32)
+            ).astype(bf)
+        second_sums[h, 2] = (
+            both(phase, h, above, 2) + first_land[phase, h, 3, 0].astype(f32)
+        ).astype(bf)
+        slot = comm.slots(2)
         out = []
-        for step in range(1, teams):
-            g = peer(step)
-
-            @pl.loop(0, heads)
-            def _(h):
-                for m in range(3):
-                    sums[g, m, h] = (
-                        gp[g, core, m, h].astype(jnp.float32)
-                        + pair[phase, g, m, h].astype(jnp.float32)
-                    ).astype(jnp.bfloat16)
-
-        for step in range(1, teams):
-            g = peer(step)
-            copy = comm.make(first + step, sums.at[g], ring.at[phase, step], same(g))
+        for k, (peer, ms) in enumerate(((to_x, via_y), (to_y, via_x))):
+            copy = comm.make(
+                slot + k, second_sums.at[h, ms], second_land.at[phase, h, ms], peer
+            )
             copy.start()
             out.append(copy)
         return out
 
-    def total_of(phase, m, h):
-        total = gp[group, core, m, h].astype(jnp.float32) + pair[phase, group, m, h].astype(
-            jnp.float32
-        )
-        for step in range(1, teams):
-            total = total + ring[phase, step, m, h].astype(jnp.float32)
-        return total
+    def total_of(phase, h, m):
+        got = first_land[phase, h, 0, m] if m < 2 else first_land[phase, h, 2, 0]
+        return (
+            both(phase, h, group, m) + got.astype(f32) + second_land[phase, h, m].astype(f32)
+        )
 
     def exchange(s):
         first = comm.slots(parts)
@@ -470,101 +566,87 @@
             copy.wait()
         squares = 0.0
         for step in range(parts):
-            x = land[s, step].astype(jnp.float32)
+            x = land[s, step].astype(f32)
             squares = squares + jnp.sum(x * x, -1, keepdims=True)
         scale = lax.rsqrt(squares / (parts * width) + EPS)
         for step in range(parts):
             z = lax.rem(mine + parts - step, parts)
             cols = pl.ds(pl.multiple_of(z * width, 128), width)
-            x = land[s, step].astype(jnp.float32)
-            mixed[s, :, cols] = (x * scale * gain[:, cols]).astype(jnp.bfloat16)
-
-    keys0 = halo(0, 0)
-    grads(wb, 0)
-    copies = pair_send(0)
-    forward(wb, 0)
-    copies = ring_send(0, copies)
-    values0 = halo(1, 0)
-    for copy in copies:
-        copy.wait()
-
-    @pl.loop(0, heads)
-    def _(h):
-        for m in range(3):
-            full[me, m, h] = total_of(0, m, h).astype(jnp.bfloat16)
-
-    first = comm.slots(2 * teams)
-    gathers = []
-    for step in range(1, teams):
-        copy = comm.make(first + step, full.at[me], full.at[me], same(peer(step)))
-        copy.start()
-        gathers.append(copy)
-    near_copy = comm.make(first + teams, full.at[me], full.at[me], partner)
-    near_copy.start()
-    later = [halo(t, 1) for t in range(2)]
-    keys0.wait_recv()
-    values0.wait_recv()
-    swaps = [swap(t, 0) for t in range(2)]
-    for copy in swaps:
-        copy.wait_recv()
-    attention(0)
-    mixing0 = exchange(0)
-    forwards = []
-    for step in range(1, teams):
-        gathers[step - 1].wait_recv()
-        block = source(step) * 2 + core
-        copy = comm.make(first + teams + step, full.at[block], full.at[block], partner)
-        copy.start()
-        forwards.append(copy)
-    near_copy.wait()
-    for copy in gathers:
-        copy.wait_send()
-    for copy in forwards:
-        copy.wait()
-
-    @pl.loop(0, heads)
-    def _(h):
+            x = land[s, step].astype(f32)
+            mixed[s, :, cols] = (x * scale * gain[:, cols]).astype(bf)
+
+    def renorm(h):
         for m in range(3):
             before, after = 0.0, 0.0
             for j in range(n):
-                w = wb[j, m, h].astype(jnp.float32)
-                t = w - full[j, m, h].astype(jnp.float32)
+                w = start[h, j, m].astype(f32)
+                t = w - full[h, j, m].astype(f32)
                 before = before + jnp.sum(w * w, 0, keepdims=True)
                 after = after + jnp.sum(t * t, 0, keepdims=True)
             goal = jnp.sqrt(before + EPS)
-            target[m, h] = goal
+            target[h, m] = goal
             ratio = goal / jnp.sqrt(after + EPS)
-            past = full[me, m, h].astype(jnp.float32)
-            moment[m, h] = past
-            weights[m, h] = (wb[me, m, h].astype(jnp.float32) - past) * ratio
+            past = full[h, me, m].astype(f32)
+            moment[h, m] = past
+            weights[h, m] = (start[h, me, m].astype(f32) - past) * ratio
             for j in range(n):
-                w = wb[j, m, h].astype(jnp.float32)
-                t = w - full[j, m, h].astype(jnp.float32)
-                full[j, m, h] = (t * ratio).astype(jnp.bfloat16)
-
-    grads(full, 1)
-    copies = pair_send(1)
+                w = start[h, j, m].astype(f32)
+                t = w - full[h, j, m].astype(f32)
+                full[h, j, m] = (t * ratio).astype(bf)
+
+    each = range(heads)
+    states = []
+    for h in each:
+        start[h, me] = shard[h]
+        states.append(gather_start(start, h, shard.at[h]))
+    for h in each:
+        gather_relay(start, h, states[h])
+    halo(0)
+    pairs = []
+    for h in each:
+        gather_end(start, h, states[h])
+        grads(start, 0, h)
+        pairs.append(pair_send(0, h))
+    firsts = [reduce_first(0, h, pairs[h]) for h in each]
+    forward(start, 0)
+    halo_relay(0)
+    seconds = [reduce_second(0, h, firsts[h]) for h in each]
+    halo_swap(0)
+    attention(0)
+    mixing0 = exchange(0)
+    states = []
+    for h in each:
+        for copy in seconds[h]:
+            copy.wait()
+        for m in range(3):
+            full[h, me, m] = total_of(0, h, m).astype(bf)
+        states.append(gather_start(full, h, full.at[h, me]))
+    for h in each:
+        gather_relay(full, h, states[h])
+    halo(1)
+    pairs = []
+    for h in each:
+        gather_end(full, h, states[h])
+        renorm(h)
+        grads(full, 1, h)
+        pairs.append(pair_send(1, h))
+    firsts = [reduce_first(1, h, pairs[h]) for h in each]
     forward(full, 1)
-    copies = ring_send(1, copies)
-    for copy in later:
-        copy.wait_recv()
-    swaps = [swap(t, 1) for t in range(2)]
-    for copy in swaps:
-        copy.wait_recv()
+    halo_relay(1)
+    seconds = [reduce_second(1, h, firsts[h]) for h in each]
+    finish(0, mixing0)
+    halo_swap(1)
     attention(1)
     mixing1 = exchange(1)
-    finish(0, mixing0)
-    for copy in copies:
-        copy.wait()
-
-    @pl.loop(0, heads)
-    def _(h):
+    for h in each:
+        for copy in seconds[h]:
+            copy.wait()
         for m in range(3):
-            momentum = BETA * moment[m, h] + total_of(1, m, h)
-            moment[m, h] = momentum
-            trial = weights[m, h] - momentum
-            weights[m, h] = trial
-            sq[m, h] = jnp.sum(trial * trial, 0, keepdims=True)
+            momentum = BETA * moment[h, m] + total_of(1, h, m)
+            moment[h, m] = momentum
+            trial = weights[h, m] - momentum
+            weights[h, m] = trial
+            sq[h, m] = jnp.sum(trial * trial, 0, keepdims=True)
 
     first = comm.slots(n)
     copies = []
@@ -577,46 +659,47 @@
     finish(1, mixing1)
     for copy in copies:
         copy.wait()
-
-    @pl.loop(0, heads)
-    def _(h):
+    for h in each:
         for m in range(3):
-            squares = sq[m, h]
+            squares = sq[h, m]
             for step in range(1, n):
-                squares = squares + sqland[step, m, h]
-            weights[m, h] = weights[m, h] * (target[m, h] / jnp.sqrt(squares + EPS))
-
-    for copy in pending:
-        copy.wait_send()
-
-
-def run_blocks(fq, fk, fv, rates, aq, ak, av, wb, gain):
+                squares = squares + sqland[step, h, m]
+            weights[h, m] = weights[h, m] * (target[h, m] / jnp.sqrt(squares + EPS))
+    for s in range(stretches):
+        halo_sent(s)
+
+
+def run_blocks(fq, fk, fv, rates, aq, ak, av, shard, gain):
     n, parts = lax.axis_size("aa"), lax.axis_size("ba")
     stretches, rows, width = fq.shape
-    heads, r, depth = wb.shape[2:]
+    heads, _, r, depth = shard.shape
     teams = n // 2
     vmem = pl.BlockSpec(memory_space=pltpu.VMEM)
-    shard = (3, heads, r, depth)
-    small = (3, heads, 1, depth)
+    piece = (3, r, depth)
+    small = (heads, 3, 1, depth)
     bf, f32 = jnp.bfloat16, jnp.float32
-    slots = 4 * stretches + 2 * (2 * teams) + 2 * teams + 2 * parts + n
+    slots = 5 * stretches + heads * 2 * (9 + 1 + 3 + 2) + 2 * parts + n
     return pl.pallas_call(
         functools.partial(block_kernel, n, parts),
         in_specs=[vmem] * 9,
         out_specs=(vmem,) * 3,
         out_shape=(
             jax.ShapeDtypeStruct((stretches, rows // parts, width * parts), bf),
-            jax.ShapeDtypeStruct(shard, f32),
-            jax.ShapeDtypeStruct(shard, f32),
+            jax.ShapeDtypeStruct((heads,) + piece, f32),
+            jax.ShapeDtypeStruct((heads,) + piece, f32),
         ),
         scratch_shapes=[
-            pltpu.VMEM((teams, 2) + shard, bf),
-            pltpu.VMEM((2, teams) + shard, bf),
-            pltpu.VMEM((teams,) + shard, bf),
-            pltpu.VMEM((2, teams) + shard, bf),
-            pltpu.VMEM((n,) + shard, bf),
+            pltpu.VMEM((heads, 2, teams) + piece, bf),
+            pltpu.VMEM((2, heads, teams) + piece, bf),
+            pltpu.VMEM((heads, 4, 2, r, depth), bf),
+            pltpu.VMEM((heads,) + piece, bf),
+            pltpu.VMEM((2, heads, 4, 2, r, depth), bf),
+            pltpu.VMEM((2, heads) + piece, bf),
+            pltpu.VMEM((heads, n) + piece, bf),
+            pltpu.VMEM((heads, n) + piece, bf),
             pltpu.VMEM((2, stretches, rows, width), bf),
             pltpu.VMEM((2, stretches, rows, width), bf),
+            pltpu.VMEM((stretches, rows, width), bf),
             pltpu.VMEM((stretches, rows, width), f32),
             pltpu.VMEM((stretches, rows, width), bf),
             pltpu.VMEM((stretches, parts, rows // parts, width), bf),
@@ -630,17 +713,16 @@
             collective_id=2, has_side_effects=True, vmem_limit_bytes=67043328
         ),
         name="blocks",
-    )(fq, fk, fv, rates, aq, ak, av, wb, gain)
+    )(fq, fk, fv, rates, aq, ak, av, shard, gain)
 
 
 def local_blocks(fq, fk, fv, rates, aq, ak, av, fast_weights, gain):
     stretches, rows, _ = fq.shape
     heads = fast_weights.shape[2]
-    shard = jnp.transpose(fast_weights, (1, 2, 0, 3)).astype(jnp.bfloat16)
-    wb = lax.all_gather(shard, "aa", axis=0)
+    shard = jnp.transpose(fast_weights.astype(jnp.bfloat16), (2, 1, 0, 3))
     rate = jnp.transpose(rates.reshape(stretches, rows, heads, 3), (0, 2, 3, 1))[..., None]
-    mixed, weights, moment = run_blocks(fq, fk, fv, rate, aq, ak, av, wb, gain[None])
-    back = (2, 0, 1, 3)
+    mixed, weights, moment = run_blocks(fq, fk, fv, rate, aq, ak, av, shard, gain[None])
+    back = (2, 1, 0, 3)
     return (mixed, jnp.transpose(weights, back), jnp.transpose(moment, back))
 
 
@@ -648,7 +730,7 @@
     stretches, rows, _ = args[0].shape
     r, _, _, depth = args[7].shape
     n, parts = lax.axis_size("aa"), lax.axis_size("ba")
-    fits = r % 16 == 0 and n % 2 == 0 and n > 2 and depth % AD == 0 and stretches == 2
+    fits = r % 16 == 0 and n == 8 and depth % AD == 0 and stretches == 2
     fits = fits and 2 * rows == WINDOW and rows % (16 * parts) == 0
     return (local_blocks if fits else local)(*args)
 

time: 226 us -> 185 us (0.82)
  waiting for transfers between devices: 43.3 us -> 0 us
  Pallas kernels: 153 us -> 174 us
  between operations: 14.1 us -> 0.66 us
  local copies, waits for them, and re-layouts: 13.1 us -> 9.65 us
  other arithmetic: 2.53 us -> 0 us
    all_gather x1 -> x0, waiting for transfers between devices: 43.3 us -> none  [local_blocks(): wb = lax.all_gather(shard, 'aa', axis=0)]
    pallas_call x1, Pallas kernels: 153 us -> 174 us  [run_blocks(): pl.pallas_call(functools.partial(block_kernel, n, parts), in_specs=[vmem]...]
    all_gather x1 -> x0, local copies, waits for them, and re-layouts: 5.66 us -> none  [local_blocks(): wb = lax.all_gather(shard, 'aa', axis=0)]
    convert_element_type x1 -> x0, other arithmetic: 2.53 us -> none  [local_blocks(): shard = jnp.transpose(fast_weights, (1, 2, 0, 3)).astype(jnp.bfloat16)]
    unnamed x9 -> x10, local copies, waits for them, and re-layouts: 5.78 us -> 7.97 us
  transfers between devices with their start and end apart: 1 -> 0, of which waited for: 1 -> 0; matrix products, arithmetic and copies ran while one was open for 1% -> 0% of each run, Pallas kernels for 0% -> 0%
where the time goes in v2:
time: 185 us
  Pallas kernels  174 us (94%)
  local copies, waits for them, and re-layouts  9.65 us (5%)
    pallas_call x1, Pallas kernels, run_blocks(): pl.pallas_call(functools.partial(block_kernel, n, parts), in_specs=[vmem]...  174 us
    unnamed x10, local copies, waits for them, and re-layouts  7.97 us

profile of v2, /device:TPU:0, one launch (start us, length us, event | category | flops | bytes accessed | tf_op | source)
XLA Modules:
  0.0 184.5 jit_solution(10607324744053090842)
XLA Ops:
  0.6 0.0 copy-start.2
  0.6 2.2 %copy.26 = bf16[80,3,2,640]{3,0,1,2:T(8,128)(2,1)} copy(f32[80,3,2,640]{3,2,1,0:T(2,128)} %param.16) | data formatting | bytes 1843200 | tf_op args[7]
  2.8 0.0 copy-done.2
  2.8 1.7 copy.18.rate
  4.5 174.2 %blocks.1 = (bf16[2,64,5120]{2,1,0:T(8,128)(2,1)}, f32[2,3,80,640]{3,2,1,0:T(8,128)}, f32[2,3,80,640]{3,2,1,0:T(8,128)}) custom-call(bf16[2,256,1280]{2,1,0:T(8,128)(2,1)} %fq.1, bf16[2,256,1280]{2,1,0:T(8,128)(2,1)} %fk.1, bf16[2,256,1280]{2,1,0:T(8,128)(2,1)} %fv.1, f32[2,2,3,256,1]{4,3,2,1,0:T(8,128)} %copy.18.rate, bf16[2,256,1280]{2,1,0:T(8,128)(2,1)} %aq.1, ...), custom_call_target="tpu_custom_call" | custom-call | tf_op jit(solution)/shard_map/blocks/pallas_call | solution.py:682
  178.7 0.0 copy-start.1
  178.8 3.0 %copy.19 = f32[80,3,2,640]{3,2,1,0:T(2,128)} copy(f32[80,3,2,640]{3,0,1,2:T(8,128)} %bitcast.13) | data formatting | bytes 2457600
  181.8 0.0 copy-done.1
  181.8 0.0 copy-start
  181.8 1.7 copy.20
  183.5 0.0 copy-done
  183.5 1.1 copy.28
Async XLA Ops:
  0.6 2.2 %copy-start.2 = (f32[2,256,6]{1,0,2:T(2,128)S(1)}, f32[2,256,6]{1,0,2:T(2,128)}, u32[]{:S(2)}) copy-start(f32[2,256,6]{1,0,2:T(2,128)} %param.12) | copy-start | bytes 36868
  178.7 3.1 %copy-start.1 = (f32[2,3,80,640]{3,2,1,0:T(8,128)S(1)}, f32[2,3,80,640]{3,2,1,0:T(8,128)}, u32[]{:S(2)}) copy-start(f32[2,3,80,640]{3,2,1,0:T(8,128)} %get-tuple-element.8) | copy-start | bytes 3686404
  181.8 1.7 copy-start

commit v3 on v2

--- a/solution.py
+++ b/solution.py
@@ -371,8 +371,7 @@
                 comm.make(slot, far.at[t, s], near.at[t, s], partner).start()
 
             copies.append(comm.make(slot, held[t].at[s], near.at[t, s], partner))
-        for copy in copies:
-            copy.wait()
+        return copies
 
     def halo_sent(s):
         for t in range(2):
@@ -609,11 +608,8 @@
         pairs.append(pair_send(0, h))
     firsts = [reduce_first(0, h, pairs[h]) for h in each]
     forward(start, 0)
+    seconds = [reduce_second(0, h, firsts[h]) for h in each]
     halo_relay(0)
-    seconds = [reduce_second(0, h, firsts[h]) for h in each]
-    halo_swap(0)
-    attention(0)
-    mixing0 = exchange(0)
     states = []
     for h in each:
         for copy in seconds[h]:
@@ -624,6 +620,7 @@
     for h in each:
         gather_relay(full, h, states[h])
     halo(1)
+    moves = halo_swap(0)
     pairs = []
     for h in each:
         gather_end(full, h, states[h])
@@ -632,12 +629,18 @@
         pairs.append(pair_send(1, h))
     firsts = [reduce_first(1, h, pairs[h]) for h in each]
     forward(full, 1)
+    for copy in moves:
+        copy.wait()
+    attention(0)
+    mixing0 = exchange(0)
     halo_relay(1)
     seconds = [reduce_second(1, h, firsts[h]) for h in each]
-    finish(0, mixing0)
-    halo_swap(1)
+    moves = halo_swap(1)
+    for copy in moves:
+        copy.wait()
     attention(1)
     mixing1 = exchange(1)
+    finish(0, mixing0)
     for h in each:
         for copy in seconds[h]:
             copy.wait()

time: 185 us -> 187 us (1.011)
  Pallas kernels: 174 us -> 176 us
    pallas_call x1, Pallas kernels: 174 us -> 176 us  [run_blocks(): pl.pallas_call(functools.partial(block_kernel, n, parts), in_specs=[vmem]...]
where the time goes in v3:
time: 187 us; the launch traced here: 186 us
  Pallas kernels  176 us (94%)
  local copies, waits for them, and re-layouts  9.65 us (5%)
    pallas_call x1, Pallas kernels, run_blocks(): pl.pallas_call(functools.partial(block_kernel, n, parts), in_specs=[vmem]...  176 us
    unnamed x10, local copies, waits for them, and re-layouts  7.97 us

profile of v3, /device:TPU:0, one launch (start us, length us, event | category | flops | bytes accessed | tf_op | source)
XLA Modules:
  0.0 186.4 jit_solution(2465350116634772782)
XLA Ops:
  0.6 0.0 copy-start.2
  0.6 2.2 %copy.26 = bf16[80,3,2,640]{3,0,1,2:T(8,128)(2,1)} copy(f32[80,3,2,640]{3,2,1,0:T(2,128)} %param.16) | data formatting | bytes 1843200 | tf_op args[7]
  2.8 0.0 copy-done.2
  2.8 1.7 copy.18.rate
  4.5 176.1 %blocks.1 = (bf16[2,64,5120]{2,1,0:T(8,128)(2,1)}, f32[2,3,80,640]{3,2,1,0:T(8,128)}, f32[2,3,80,640]{3,2,1,0:T(8,128)}) custom-call(bf16[2,256,1280]{2,1,0:T(8,128)(2,1)} %fq.1, bf16[2,256,1280]{2,1,0:T(8,128)(2,1)} %fk.1, bf16[2,256,1280]{2,1,0:T(8,128)(2,1)} %fv.1, f32[2,2,3,256,1]{4,3,2,1,0:T(8,128)} %copy.18.rate, bf16[2,256,1280]{2,1,0:T(8,128)(2,1)} %aq.1, ...), custom_call_target="tpu_custom_call" | custom-call | tf_op jit(solution)/shard_map/blocks/pallas_call | solution.py:685
  180.6 0.0 copy-start.1
  180.6 3.0 %copy.19 = f32[80,3,2,640]{3,2,1,0:T(2,128)} copy(f32[80,3,2,640]{3,0,1,2:T(8,128)} %bitcast.13) | data formatting | bytes 2457600
  183.7 0.0 copy-done.1
  183.7 0.0 copy-start
  183.7 1.7 copy.20
  185.4 0.0 copy-done
  185.4 1.1 copy.28
Async XLA Ops:
  0.6 2.2 %copy-start.2 = (f32[2,256,6]{1,0,2:T(2,128)S(1)}, f32[2,256,6]{1,0,2:T(2,128)}, u32[]{:S(2)}) copy-start(f32[2,256,6]{1,0,2:T(2,128)} %param.12) | copy-start | bytes 36868
  180.6 3.1 %copy-start.1 = (f32[2,3,80,640]{3,2,1,0:T(8,128)S(1)}, f32[2,3,80,640]{3,2,1,0:T(8,128)}, u32[]{:S(2)}) copy-start(f32[2,3,80,640]{3,2,1,0:T(8,128)} %get-tuple-element.8) | copy-start | bytes 3686404
  183.7 1.7 copy-start
